TPU v7x, 512 devices: a whole 4x4x16 slice. The times are simulated.
512 devices in a mesh: band: 64 (over x_lo, z, core), tile: 8 (over y, x_hi).
Axes of the slice: x: 4 (x_hi: 2, x_lo: 2; x = x_hi * 2 + x_lo), y: 4, z: 16, core: 2. Of those that a mesh axis runs over, the one named last changes fastest.
Arguments:
- alm: bfloat16 [1024, 9, 2, 1024], P('band', None, None, 'tile'), may hold values from -22 to 22
- legendre: bfloat16 [1024, 1024, 1024], P('band', 'tile'), may hold values from -0.1875 to 0.1875
- order_of_slot: int32 [1024], replicated, may hold values from 0 to 1023, each once
Outputs:
- ilc_map: float32 [1024, 4096], P('band', 'tile')
- ilc_alm: float32 [1024, 2, 1024], P('band', None, 'tile')
Inputs may be any that keep to these rules, and one draw needn't show every extreme that they name: `order_of_slot`: every order 0 to 1023 stands in exactly one slot.
All inputs are finite; a program needn't handle non-finite values.
Results may differ from a plain program's by a relative error of at most 0.02.
Values may be sent and summed in bfloat16 or wider, within the bound.
A program may use at most 64 MiB of HBM per device.

v0:
```python
import math
import jax
import jax.numpy as jnp
from jax import lax
from jax.sharding import PartitionSpec as P

C = 9
L = 1024
NLON = 4096
RB = 16
HALO = 32
RIDGE = 0.1
EPSILON = 1e-06


def sent_to_all(value, axis):
    copies = jnp.broadcast_to(value, (lax.axis_size(axis), *value.shape))
    return lax.all_to_all(copies, axis, split_axis=0, concat_axis=0, tiled=True)


def taken_together(value, axis):
    return sent_to_all(value, axis).astype(jnp.float32).sum(axis=0)


def with_halo(block, sides, width):
    for axis, dim in sides:
        count = lax.axis_size(axis)
        forward = [(i, i + 1) for i in range(count - 1)]
        forward.append((count - 1, 0))
        backward = [(target, source) for source, target in forward]
        low = lax.ppermute(
            lax.slice_in_dim(block, block.shape[dim] - width, None, axis=dim), axis, forward
        )
        high = lax.ppermute(lax.slice_in_dim(block, 0, width, axis=dim), axis, backward)
        block = jnp.concatenate([low, block, high], axis=dim)
    return block


def taken_together_2(value, axis):
    everything = sent_to_all(value, axis)
    return jnp.sum(everything, axis=0)


def make_basis(order_of_slot, begin_at, cell_count):
    columns = begin_at + jnp.arange(cell_count, dtype=jnp.int32)
    phases = order_of_slot[:, None] * columns[None, :] % NLON
    angles = phases.astype(jnp.float32) * (2.0 * math.pi / NLON)
    scaling = 1.0 / math.sqrt(L)
    return jnp.stack([jnp.cos(angles) * scaling, -jnp.sin(angles) * scaling]).astype(jnp.bfloat16)


def pair_table():
    return [(a_at, b_at) for a_at in range(C) for b_at in range(a_at, C)]


def window_sum(products):
    span_cells = products.shape[2]
    width_cells = span_cells - 2 * HALO
    total = products
    span = 1
    while span < 2 * HALO:
        total = total[:, :, :-span] + total[:, :, span:]
        span = span * 2
    return total[:, :, :width_cells] + products[:, :, 2 * HALO : 2 * HALO + width_cells]


def smooth_pairs(padded):
    widened = padded.astype(jnp.float32)
    products = jnp.stack([widened[a_at] * widened[b_at] for a_at, b_at in pair_table()])
    return window_sum(products) / (2 * HALO + 1)


def solve_weights(smoothed):
    entries = {}
    for pair_at, (a_at, b_at) in enumerate(pair_table()):
        entries[a_at, b_at] = smoothed[pair_at]
    trace_mean = entries[0, 0]
    for chan_at in range(1, C):
        trace_mean = trace_mean + entries[chan_at, chan_at]
    ridge_term = RIDGE * (trace_mean / C + EPSILON)
    factor = {}
    for row_at in range(C):
        for col_at in range(row_at + 1):
            running = entries[col_at, row_at]
            if row_at == col_at:
                running = running + ridge_term
            for inner_at in range(col_at):
                running = running - factor[row_at, inner_at] * factor[col_at, inner_at]
            if row_at == col_at:
                factor[row_at, row_at] = jnp.sqrt(running)
            else:
                factor[row_at, col_at] = running / factor[col_at, col_at]
    forward = []
    for row_at in range(C):
        running = jnp.ones_like(ridge_term)
        for inner_at in range(row_at):
            running = running - factor[row_at, inner_at] * forward[inner_at]
        forward.append(running / factor[row_at, row_at])
    backward = [forward[0]] * C
    for row_at in reversed(range(C)):
        running = forward[row_at]
        for inner_at in range(row_at + 1, C):
            running = running - factor[inner_at, row_at] * backward[inner_at]
        backward[row_at] = running / factor[row_at, row_at]
    normal = backward[0]
    for chan_at in range(1, C):
        normal = normal + backward[chan_at]
    return jnp.stack([solved / normal for solved in backward])


def to_band_layout(parts):
    return lax.all_to_all(parts, "band", split_axis=3, concat_axis=0, tiled=True)


def body(alm, legendre, order_of_slot):
    tile_count = lax.axis_size("tile")
    band_count = lax.axis_size("band")
    tile_at = lax.axis_index("tile")
    slot_count = alm.shape[0]
    lon_cells = NLON // tile_count
    partial_value = jnp.einsum("scel,slr->scer", alm, legendre, preferred_element_type=jnp.float32)
    own_basis = make_basis(order_of_slot, tile_at * lon_cells, lon_cells)
    shaped = partial_value.astype(jnp.bfloat16).reshape(slot_count, C, 2, band_count, RB)
    gathered = to_band_layout(shaped)
    summed = taken_together(gathered.astype(jnp.float32).astype(jnp.bfloat16), "tile").astype(
        jnp.float32
    )
    cycle_modes = summed.astype(jnp.bfloat16).reshape(L, C, 2, RB)
    channel_maps = jnp.einsum(
        "scer,esx->crx", cycle_modes, own_basis, preferred_element_type=jnp.float32
    ).astype(jnp.bfloat16)
    padded = with_halo(channel_maps, (("tile", 2),), HALO)
    weights = solve_weights(smooth_pairs(padded))
    ilc_map = jnp.sum(weights * channel_maps.astype(jnp.float32), axis=0)
    map_low = ilc_map.astype(jnp.bfloat16)
    cycle_partial = jnp.einsum(
        "rx,esx->res", map_low, own_basis, preferred_element_type=jnp.float32
    )
    routed = lax.all_to_all(cycle_partial, "band", split_axis=2, concat_axis=0, tiled=True)
    cycle_spectra = taken_together_2(routed, "tile").astype(jnp.bfloat16)
    ilc_alm = jnp.einsum(
        "slr,res->sel", legendre, cycle_spectra, preferred_element_type=jnp.float32
    )
    return (ilc_map, ilc_alm)


def solution(mesh):
    placed = (P("band", None, None, "tile"), P("band", "tile", None), P())
    return jax.shard_map(
        body,
        mesh=mesh,
        in_specs=placed,
        out_specs=(P("band", "tile"), P("band", None, "tile")),
        check_vma=False,
    )
```

profile of v0, /device:TPU:1, one launch (start us, length us, event | category | flops | bytes accessed | tf_op | source)
XLA Modules:
  0.0 249.8 jit_solution(7399007213763697263)
XLA Ops:
  0.6 2.9 %fusion.7 = bf16[16,9,2,1024]{3,1,2,0:T(8,128)(2,1)S(1)} fusion(bf16[16,128,1024]{2,1,0:T(8,128)(2,1)} %param.4, bf16[16,9,2,128]{3,2,1,0:T(2,128)(2,1)} %param.3), kind=kOutput, calls=%fused_computation.20 | convolution fusion | flops 75792384 | bytes 4857856 | tf_op jit(solution)/shard_map/scel,slr->scer/dot_general | solution.py:121
  3.5 4.9 %reshape.154 = bf16[16,9,2,64,16]{4,3,1,2,0:T(8,128)(2,1)} reshape(bf16[16,9,2,1024]{3,1,2,0:T(8,128)(2,1)S(1)} %fusion.7) | data formatting | bytes 1179648 | tf_op jit(solution)/shard_map/reshape | solution.py:123
  8.5 7.5 %copy.40 = bf16[16,9,2,64,16]{4,0,2,1,3:T(8,128)(2,1)} copy(bf16[16,9,2,64,16]{4,3,1,2,0:T(8,128)(2,1)} %reshape.154) | data formatting | bytes 1179648 | tf_op jit(solution)/shard_map/reshape | solution.py:123
  16.0 6.6 %reshape.155 = bf16[64,2,2304]{2,1,0:T(2,128)(2,1)S(1)} reshape(bf16[64,9,2,16,16]{4,3,2,1,0:T(8,128)(2,1)} %bitcast.50) | data formatting | bytes 1179648
  22.6 52.0 %all_to_all.46 = bf16[64,2,2304]{2,1,0:T(2,128)(2,1)S(1)} all-to-all(bf16[64,2,2304]{2,1,0:T(2,128)(2,1)S(1)} %reshape.155), channel_id=1, replica_groups=mesh['band'=64,'tile'=8] {'band'}, dimensions={0} | all-to-all | bytes 1179648 | tf_op jit(solution)/shard_map/all_to_all | solution.py:112
  74.7 4.7 %reshape.156 = bf16[64,9,2,16,16]{4,3,2,1,0:T(8,128)(2,1)} reshape(bf16[64,2,2304]{2,1,0:T(2,128)(2,1)S(1)} %all_to_all.46) | data formatting | bytes 1179648
  79.4 5.3 %bitcast_bitcast_fusion = bf16[64,16,9,2,1,16]{5,1,3,2,0,4:T(8,128)(2,1)} fusion(bf16[64,9,2,16,16]{4,3,2,1,0:T(8,128)(2,1)} %reshape.156), kind=kLoop, calls=%fused_computation.250 | loop fusion | bytes 1179648 | tf_op jit(solution)/shard_map/all_to_all | solution.py:112
  84.7 9.8 %copy.22 = bf16[64,16,9,2,1,16]{1,0,5,3,2,4:T(8,128)(2,1)} copy(bf16[64,16,9,2,1,16]{5,1,3,2,0,4:T(8,128)(2,1)} %bitcast_bitcast_fusion) | data formatting | bytes 1179648 | tf_op jit(solution)/shard_map/all_to_all | solution.py:112
  94.5 8.9 %all_to_all.35 = bf16[1024,9,2,16]{0,3,2,1:T(8,128)(2,1)S(1)} reshape(bf16[64,16,9,2,1,16]{1,0,5,3,2,4:T(8,128)(2,1)} %copy.22) | data formatting | bytes 1179648 | tf_op jit(solution)/shard_map/all_to_all | solution.py:112
  103.3 2.8 %broadcast_in_dim.8 = bf16[8,1024,9,2,1,16]{1,5,4,3,2,0:T(8,128)(2,1)} broadcast(bf16[1024,9,2,16]{0,3,2,1:T(8,128)(2,1)S(1)} %all_to_all.35), dimensions={1,2,3,5} | broadcast | bytes 5308416 | tf_op jit(solution)/shard_map/broadcast_in_dim | solution.py:17
  106.1 6.5 %all-to-all-start.1 = ((bf16[8,1024,9,2,1,16]{1,5,4,3,2,0:T(8,128)(2,1)}), bf16[8,1024,9,2,1,16]{1,5,4,3,2,0:T(8,128)(2,1)}, u32[]{:S(2)}, u32[]{:S(2)}) async-start(bf16[8,1024,9,2,1,16]{1,5,4,3,2,0:T(8,128)(2,1)} %broadcast_in_dim.8), calls=%async_computation.1 | async-start | bytes 9437184 | tf_op jit(solution)/shard_map/all_to_all | solution.py:18
  112.6 9.2 %multiply_convert_fusion.1 = (bf16[1,1024,512]{2,1,0:T(8,128)(2,1)S(1)}, bf16[1,1024,512]{2,1,0:T(8,128)(2,1)S(1)}) fusion(s32[512]{0:T(512)S(1)} %iota_add_fusion, s32[1024]{0:T(1024)S(1)} %copy-done.1), kind=kLoop, calls=%fused_computation.14 | loop fusion | flops 9961472 | bytes 2103296 | tf_op jit(solution)/shard_map/convert.1
  121.8 47.6 %all-to-all-done.1 = bf16[8,1024,9,2,1,16]{1,5,4,3,2,0:T(8,128)(2,1)} async-done(((bf16[8,1024,9,2,1,16]{1,5,4,3,2,0:T(8,128)(2,1)}), bf16[8,1024,9,2,1,16]{1,5,4,3,2,0:T(8,128)(2,1)}, u32[]{:S(2)}, u32[]{:S(2)}) %all-to-all-start.1) | async-done | bytes 4718624 | tf_op jit(solution)/shard_map/all_to_all | solution.py:18
  169.4 3.4 %reduce_sum.30 = bf16[1024,9,2,16]{0,3,2,1:T(8,128)(2,1)S(1)} reduce(bf16[8,1024,9,2,1,16]{1,5,4,3,2,0:T(8,128)(2,1)} %all-to-all-done.1, bf16[]{:T(256)} %constant.12.clone.1), dimensions={0,4}, to_apply=%region_0.1 | reduce | flops 2064384 | bytes 5308418 | tf_op jit(solution)/shard_map/reduce_sum | solution.py:22
  173.4 3.3 %collective-permute-start.1 = (bf16[9,16,32]{2,1,0:T(8,128)(2,1)S(1)}, bf16[9,16,32]{2,1,0:T(8,128)(2,1)S(1)}, u32[]{:S(2)}, u32[]{:S(2)}) collective-permute-start(bf16[9,16,32]{2,1,0:T(8,128)(2,1)S(1)} %get-tuple-element.14), channel_id=1, source_target_pairs={{1,0},{2,1},{3,2},{4,3},{5,4},{6,5},{7,6},{0,7},{9,8},{10,9},{11,1... | collective-permute-start | bytes 27656 | tf_op jit(solution)/shard_map/ppermute | solution.py:34
  176.7 3.7 %collective-permute-start = (bf16[9,16,32]{2,1,0:T(8,128)(2,1)S(1)}, bf16[9,16,32]{2,1,0:T(8,128)(2,1)S(1)}, u32[]{:S(2)}, u32[]{:S(2)}) collective-permute-start(bf16[9,16,32]{2,1,0:T(8,128)(2,1)S(1)} %get-tuple-element.13), channel_id=1, source_target_pairs={{0,1},{1,2},{2,3},{3,4},{4,5},{5,6},{6,7},{7,0},{8,9},{9,10},{10,1... | collective-permute-start | bytes 27656 | tf_op jit(solution)/shard_map/ppermute | solution.py:31
  180.4 4.6 %collective-permute-done = bf16[9,16,32]{2,1,0:T(8,128)(2,1)S(1)} collective-permute-done((bf16[9,16,32]{2,1,0:T(8,128)(2,1)S(1)}, bf16[9,16,32]{2,1,0:T(8,128)(2,1)S(1)}, u32[]{:S(2)}, u32[]{:S(2)}) %collective-permute-start) | collective-permute-done | bytes 9248 | tf_op jit(solution)/shard_map/ppermute | solution.py:31
  189.7 0.7 multiply_subtract_fusion
  196.4 1.4 reshape.157
  197.9 24.3 %all_to_all.47 = f32[64,1,512]{2,1,0:T(1,128)S(1)} all-to-all(f32[64,1,512]{2,1,0:T(1,128)S(1)} %reshape.157), channel_id=1, replica_groups=mesh['band'=64,'tile'=8] {'band'}, dimensions={0} | all-to-all | bytes 262144 | tf_op jit(solution)/shard_map/all_to_all | solution.py:139
  222.7 0.9 reduce.2
  223.7 1.4 reshape.158
  226.4 19.3 %all_to_all.48 = f32[8,1024,2,16]{1,3,2,0:T(8,128)S(1)} all-to-all(f32[8,1024,2,16]{1,3,2,0:T(8,128)S(1)} %broadcast_in_dim.9), channel_id=1, replica_groups=mesh['band'=64,'tile'=8] {'tile'}, dimensions={0} | all-to-all | bytes 2097152 | tf_op jit(solution)/shard_map/all_to_all | solution.py:18
  245.8 4.0 %fusion.19 = f32[16,2,128]{2,1,0:T(2,128)} fusion(bf16[16,128,1024]{2,1,0:T(8,128)(2,1)} %param.4, bf16[1024,2,16]{0,2,1:T(8,128)(2,1)S(1)} %reduce_sum.32), kind=kOutput, calls=%fused_computation.85 | convolution fusion | flops 8388608 | bytes 4276224 | tf_op jit(solution)/shard_map/slr,res->sel/dot_general | solution.py:141
  (78 shorter events, 12.7 us)
Async XLA Ops:
  106.1 6.5 %copy-start.1 = (s32[1024]{0:T(1024)S(1)}, s32[1024]{0:T(1024)}, u32[]{:S(2)}) copy-start(s32[1024]{0:T(1024)} %param.5) | copy-start | bytes 12292
  106.1 63.3 %all-to-all-start.1 = ((bf16[8,1024,9,2,1,16]{1,5,4,3,2,0:T(8,128)(2,1)}), bf16[8,1024,9,2,1,16]{1,5,4,3,2,0:T(8,128)(2,1)}, u32[]{:S(2)}, u32[]{:S(2)}) async-start(bf16[8,1024,9,2,1,16]{1,5,4,3,2,0:T(8,128)(2,1)} %broadcast_in_dim.8), calls=%async_computation.1 | async-start | bytes 9437184 | tf_op jit(solution)/shard_map/all_to_all | solution.py:18
  173.4 7.0 %collective-permute-start.1 = (bf16[9,16,32]{2,1,0:T(8,128)(2,1)S(1)}, bf16[9,16,32]{2,1,0:T(8,128)(2,1)S(1)}, u32[]{:S(2)}, u32[]{:S(2)}) collective-permute-start(bf16[9,16,32]{2,1,0:T(8,128)(2,1)S(1)} %get-tuple-element.14), channel_id=1, source_target_pairs={{1,0},{2,1},{3,2},{4,3},{5,4},{6,5},{7,6},{0,7},{9,8},{10,9},{11,1... | collective-permute-start | bytes 27656 | tf_op jit(solution)/shard_map/ppermute | solution.py:34
  176.7 8.3 %collective-permute-start = (bf16[9,16,32]{2,1,0:T(8,128)(2,1)S(1)}, bf16[9,16,32]{2,1,0:T(8,128)(2,1)S(1)}, u32[]{:S(2)}, u32[]{:S(2)}) collective-permute-start(bf16[9,16,32]{2,1,0:T(8,128)(2,1)S(1)} %get-tuple-element.13), channel_id=1, source_target_pairs={{0,1},{1,2},{2,3},{3,4},{4,5},{5,6},{6,7},{7,0},{8,9},{9,10},{10,1... | collective-permute-start | bytes 27656 | tf_op jit(solution)/shard_map/ppermute | solution.py:31
  195.2 1.2 copy-start
where the time goes:
time: 251 us; the launch traced here: 250 us
  blocking collectives  95.7 us (38%)
  local copies, waits for them, and re-layouts  56.4 us (22%)
  waiting for transfers between devices  52.1 us (21%)
  other arithmetic  22.8 us (9%)
  starting transfers between devices  13.5 us (5%)
  matrix products  8.03 us (3%)
    all_to_all x1, blocking collectives, to_band_layout(): lax.all_to_all(parts, 'band', split_axis=3, concat_axis=0, tiled=True)  52 us
    all_to_all x1, waiting for transfers between devices, sent_to_all(): return lax.all_to_all(copies, axis, split_axis=0, concat_axis=0, tiled=True)  47.6 us
    all_to_all x1, blocking collectives, body(): lax.all_to_all(cycle_partial, 'band', split_axis=2, concat_axis=0, tiled=...  24.3 us
    all_to_all x3, local copies, waits for them, and re-layouts, to_band_layout(): lax.all_to_all(parts, 'band', split_axis=3, concat_axis=0, tiled=True)  23.9 us
    all_to_all x1, blocking collectives, sent_to_all(): return lax.all_to_all(copies, axis, split_axis=0, concat_axis=0, tiled=True)  19.3 us
    unnamed x8, local copies, waits for them, and re-layouts  14.2 us
    reshape x2, local copies, waits for them, and re-layouts, body(): partial_value.astype(jnp.bfloat16).reshape(slot_count, C, 2, band_count, RB)  12.5 us
    another operation x1, other arithmetic  9.19 us
  transfers between devices with their start and end apart: 3, of which 2 were waited for; matrix products, arithmetic and copies ran while one was open for 4% of the time, Pallas kernels for 0%

commit v1 on v0

--- a/solution.py
+++ b/solution.py
@@ -136,7 +136,12 @@
     cycle_partial = jnp.einsum(
         "rx,esx->res", map_low, own_basis, preferred_element_type=jnp.float32
     )
-    routed = lax.all_to_all(cycle_partial, "band", split_axis=2, concat_axis=0, tiled=True)
+    routed = jnp.concatenate(
+        lax.all_to_all(
+            jnp.stack(jnp.split(cycle_partial, lax.axis_size("band"), axis=2)), "band", 0, 0
+        ),
+        axis=0,
+    )
     cycle_spectra = taken_together_2(routed, "tile").astype(jnp.bfloat16)
     ilc_alm = jnp.einsum(
         "slr,res->sel", legendre, cycle_spectra, preferred_element_type=jnp.float32

time: 251 us -> 254 us (1.012)
  local copies, waits for them, and re-layouts: 56.4 us -> 60 us
    unnamed x8 -> x71, local copies, waits for them, and re-layouts: 14.2 us -> 18.5 us
where the time goes in v1:
time: 254 us; the launch traced here: 253 us
  blocking collectives  95.7 us (38%)
  local copies, waits for them, and re-layouts  60 us (24%)
  waiting for transfers between devices  52.1 us (21%)
  other arithmetic  22.8 us (9%)
  starting transfers between devices  13.5 us (5%)
  matrix products  8.03 us (3%)
    all_to_all x1, blocking collectives, to_band_layout(): lax.all_to_all(parts, 'band', split_axis=3, concat_axis=0, tiled=True)  52 us
    all_to_all x1, waiting for transfers between devices, sent_to_all(): return lax.all_to_all(copies, axis, split_axis=0, concat_axis=0, tiled=True)  47.6 us
    all_to_all x1, blocking collectives, body(): lax.all_to_all(jnp.stack(jnp.split(cycle_partial, lax.axis_size('band'),...  24.3 us
    all_to_all x3, local copies, waits for them, and re-layouts, to_band_layout(): lax.all_to_all(parts, 'band', split_axis=3, concat_axis=0, tiled=True)  23.9 us
    all_to_all x1, blocking collectives, sent_to_all(): return lax.all_to_all(copies, axis, split_axis=0, concat_axis=0, tiled=True)  19.3 us
    unnamed x71, local copies, waits for them, and re-layouts  18.5 us
    reshape x2, local copies, waits for them, and re-layouts, body(): partial_value.astype(jnp.bfloat16).reshape(slot_count, C, 2, band_count, RB)  12.5 us
    another operation x1, other arithmetic  9.19 us
  transfers between devices with their start and end apart: 3, of which 2 were waited for; matrix products, arithmetic and copies ran while one was open for 4% of the time, Pallas kernels for 0%

profile of v1, /device:TPU:1, one launch (start us, length us, event | category | flops | bytes accessed | tf_op | source)
XLA Modules:
  0.0 253.4 jit_solution(8261705352776086748)
XLA Ops:
  0.6 2.9 %fusion.7 = bf16[16,9,2,1024]{3,1,2,0:T(8,128)(2,1)S(1)} fusion(bf16[16,128,1024]{2,1,0:T(8,128)(2,1)} %param.4, bf16[16,9,2,128]{3,2,1,0:T(2,128)(2,1)} %param.3), kind=kOutput, calls=%fused_computation.20 | convolution fusion | flops 75792384 | bytes 4857856 | tf_op jit(solution)/shard_map/scel,slr->scer/dot_general | solution.py:121
  3.5 4.9 %reshape.158 = bf16[16,9,2,64,16]{4,3,1,2,0:T(8,128)(2,1)} reshape(bf16[16,9,2,1024]{3,1,2,0:T(8,128)(2,1)S(1)} %fusion.7) | data formatting | bytes 1179648 | tf_op jit(solution)/shard_map/reshape | solution.py:123
  8.5 7.5 %copy.169 = bf16[16,9,2,64,16]{4,0,2,1,3:T(8,128)(2,1)} copy(bf16[16,9,2,64,16]{4,3,1,2,0:T(8,128)(2,1)} %reshape.158) | data formatting | bytes 1179648 | tf_op jit(solution)/shard_map/reshape | solution.py:123
  16.0 6.6 %reshape.159 = bf16[64,2,2304]{2,1,0:T(2,128)(2,1)S(1)} reshape(bf16[64,9,2,16,16]{4,3,2,1,0:T(8,128)(2,1)} %bitcast.296) | data formatting | bytes 1179648
  22.6 52.0 %all_to_all.33 = bf16[64,2,2304]{2,1,0:T(2,128)(2,1)S(1)} all-to-all(bf16[64,2,2304]{2,1,0:T(2,128)(2,1)S(1)} %reshape.159), channel_id=1, replica_groups=mesh['band'=64,'tile'=8] {'band'}, dimensions={0} | all-to-all | bytes 1179648 | tf_op jit(solution)/shard_map/all_to_all | solution.py:112
  74.7 4.7 %reshape.160 = bf16[64,9,2,16,16]{4,3,2,1,0:T(8,128)(2,1)} reshape(bf16[64,2,2304]{2,1,0:T(2,128)(2,1)S(1)} %all_to_all.33) | data formatting | bytes 1179648
  79.4 5.3 %bitcast_bitcast_fusion = bf16[64,16,9,2,1,16]{5,1,3,2,0,4:T(8,128)(2,1)} fusion(bf16[64,9,2,16,16]{4,3,2,1,0:T(8,128)(2,1)} %reshape.160), kind=kLoop, calls=%fused_computation.377 | loop fusion | bytes 1179648 | tf_op jit(solution)/shard_map/all_to_all | solution.py:112
  84.7 9.8 %copy.155 = bf16[64,16,9,2,1,16]{1,0,5,3,2,4:T(8,128)(2,1)} copy(bf16[64,16,9,2,1,16]{5,1,3,2,0,4:T(8,128)(2,1)} %bitcast_bitcast_fusion) | data formatting | bytes 1179648 | tf_op jit(solution)/shard_map/all_to_all | solution.py:112
  94.5 8.9 %all_to_all.25 = bf16[1024,9,2,16]{0,3,2,1:T(8,128)(2,1)S(1)} reshape(bf16[64,16,9,2,1,16]{1,0,5,3,2,4:T(8,128)(2,1)} %copy.155) | data formatting | bytes 1179648 | tf_op jit(solution)/shard_map/all_to_all | solution.py:112
  103.3 2.8 %broadcast_in_dim.8 = bf16[8,1024,9,2,1,16]{1,5,4,3,2,0:T(8,128)(2,1)} broadcast(bf16[1024,9,2,16]{0,3,2,1:T(8,128)(2,1)S(1)} %all_to_all.25), dimensions={1,2,3,5} | broadcast | bytes 5308416 | tf_op jit(solution)/shard_map/broadcast_in_dim | solution.py:17
  106.1 6.5 %all-to-all-start.1 = ((bf16[8,1024,9,2,1,16]{1,5,4,3,2,0:T(8,128)(2,1)}), bf16[8,1024,9,2,1,16]{1,5,4,3,2,0:T(8,128)(2,1)}, u32[]{:S(2)}, u32[]{:S(2)}) async-start(bf16[8,1024,9,2,1,16]{1,5,4,3,2,0:T(8,128)(2,1)} %broadcast_in_dim.8), calls=%async_computation.1 | async-start | bytes 9437184 | tf_op jit(solution)/shard_map/all_to_all | solution.py:18
  112.6 9.2 %multiply_convert_fusion.1 = (bf16[1,1024,512]{2,1,0:T(8,128)(2,1)S(1)}, bf16[1,1024,512]{2,1,0:T(8,128)(2,1)S(1)}) fusion(s32[512]{0:T(512)S(1)} %iota_add_fusion, s32[1024]{0:T(1024)S(1)} %copy-done.1), kind=kLoop, calls=%fused_computation.14 | loop fusion | flops 9961472 | bytes 2103296 | tf_op jit(solution)/shard_map/convert.1
  121.8 47.6 %all-to-all-done.1 = bf16[8,1024,9,2,1,16]{1,5,4,3,2,0:T(8,128)(2,1)} async-done(((bf16[8,1024,9,2,1,16]{1,5,4,3,2,0:T(8,128)(2,1)}), bf16[8,1024,9,2,1,16]{1,5,4,3,2,0:T(8,128)(2,1)}, u32[]{:S(2)}, u32[]{:S(2)}) %all-to-all-start.1) | async-done | bytes 4718624 | tf_op jit(solution)/shard_map/all_to_all | solution.py:18
  169.4 3.4 %reduce_sum.30 = bf16[1024,9,2,16]{0,3,2,1:T(8,128)(2,1)S(1)} reduce(bf16[8,1024,9,2,1,16]{1,5,4,3,2,0:T(8,128)(2,1)} %all-to-all-done.1, bf16[]{:T(256)} %constant.12.clone.1), dimensions={0,4}, to_apply=%region_0.1 | reduce | flops 2064384 | bytes 5308418 | tf_op jit(solution)/shard_map/reduce_sum | solution.py:22
  173.4 3.3 %collective-permute-start.1 = (bf16[9,16,32]{2,1,0:T(8,128)(2,1)S(1)}, bf16[9,16,32]{2,1,0:T(8,128)(2,1)S(1)}, u32[]{:S(2)}, u32[]{:S(2)}) collective-permute-start(bf16[9,16,32]{2,1,0:T(8,128)(2,1)S(1)} %get-tuple-element.14), channel_id=1, source_target_pairs={{1,0},{2,1},{3,2},{4,3},{5,4},{6,5},{7,6},{0,7},{9,8},{10,9},{11,1... | collective-permute-start | bytes 27656 | tf_op jit(solution)/shard_map/ppermute | solution.py:34
  176.7 3.7 %collective-permute-start = (bf16[9,16,32]{2,1,0:T(8,128)(2,1)S(1)}, bf16[9,16,32]{2,1,0:T(8,128)(2,1)S(1)}, u32[]{:S(2)}, u32[]{:S(2)}) collective-permute-start(bf16[9,16,32]{2,1,0:T(8,128)(2,1)S(1)} %get-tuple-element.13), channel_id=1, source_target_pairs={{0,1},{1,2},{2,3},{3,4},{4,5},{5,6},{6,7},{7,0},{8,9},{9,10},{10,1... | collective-permute-start | bytes 27656 | tf_op jit(solution)/shard_map/ppermute | solution.py:31
  180.4 4.6 %collective-permute-done = bf16[9,16,32]{2,1,0:T(8,128)(2,1)S(1)} collective-permute-done((bf16[9,16,32]{2,1,0:T(8,128)(2,1)S(1)}, bf16[9,16,32]{2,1,0:T(8,128)(2,1)S(1)}, u32[]{:S(2)}, u32[]{:S(2)}) %collective-permute-start) | collective-permute-done | bytes 9248 | tf_op jit(solution)/shard_map/ppermute | solution.py:31
  189.7 0.7 multiply_subtract_fusion
  200.6 1.7 reshape.161
  202.3 24.3 %all_to_all.34 = f32[64,1,512]{2,1,0:T(1,128)S(1)} all-to-all(f32[64,1,512]{2,1,0:T(1,128)S(1)} %reshape.161), channel_id=1, replica_groups=mesh['band'=64,'tile'=8] {'band'}, dimensions={0} | all-to-all | bytes 262144 | tf_op jit(solution)/shard_map/all_to_all | solution.py:140
  227.2 0.9 reduce.2
  228.1 1.4 reshape.162
  230.1 19.3 %all_to_all.35 = f32[8,1024,2,16]{1,3,2,0:T(8,128)S(1)} all-to-all(f32[8,1024,2,16]{1,3,2,0:T(8,128)S(1)} %broadcast_in_dim.9), channel_id=1, replica_groups=mesh['band'=64,'tile'=8] {'tile'}, dimensions={0} | all-to-all | bytes 2097152 | tf_op jit(solution)/shard_map/all_to_all | solution.py:18
  249.5 4.0 %fusion.19 = f32[16,2,128]{2,1,0:T(2,128)} fusion(bf16[16,128,1024]{2,1,0:T(8,128)(2,1)} %param.4, bf16[1024,2,16]{0,2,1:T(8,128)(2,1)S(1)} %reduce_sum.32), kind=kOutput, calls=%fused_computation.148 | convolution fusion | flops 8388608 | bytes 4276224 | tf_op jit(solution)/shard_map/slr,res->sel/dot_general | solution.py:146
  (141 shorter events, 16.1 us)
Async XLA Ops:
  106.1 6.5 %copy-start.1 = (s32[1024]{0:T(1024)S(1)}, s32[1024]{0:T(1024)}, u32[]{:S(2)}) copy-start(s32[1024]{0:T(1024)} %param.5) | copy-start | bytes 12292
  106.1 63.3 %all-to-all-start.1 = ((bf16[8,1024,9,2,1,16]{1,5,4,3,2,0:T(8,128)(2,1)}), bf16[8,1024,9,2,1,16]{1,5,4,3,2,0:T(8,128)(2,1)}, u32[]{:S(2)}, u32[]{:S(2)}) async-start(bf16[8,1024,9,2,1,16]{1,5,4,3,2,0:T(8,128)(2,1)} %broadcast_in_dim.8), calls=%async_computation.1 | async-start | bytes 9437184 | tf_op jit(solution)/shard_map/all_to_all | solution.py:18
  173.4 7.0 %collective-permute-start.1 = (bf16[9,16,32]{2,1,0:T(8,128)(2,1)S(1)}, bf16[9,16,32]{2,1,0:T(8,128)(2,1)S(1)}, u32[]{:S(2)}, u32[]{:S(2)}) collective-permute-start(bf16[9,16,32]{2,1,0:T(8,128)(2,1)S(1)} %get-tuple-element.14), channel_id=1, source_target_pairs={{1,0},{2,1},{3,2},{4,3},{5,4},{6,5},{7,6},{0,7},{9,8},{10,9},{11,1... | collective-permute-start | bytes 27656 | tf_op jit(solution)/shard_map/ppermute | solution.py:34
  176.7 8.3 %collective-permute-start = (bf16[9,16,32]{2,1,0:T(8,128)(2,1)S(1)}, bf16[9,16,32]{2,1,0:T(8,128)(2,1)S(1)}, u32[]{:S(2)}, u32[]{:S(2)}) collective-permute-start(bf16[9,16,32]{2,1,0:T(8,128)(2,1)S(1)} %get-tuple-element.13), channel_id=1, source_target_pairs={{0,1},{1,2},{2,3},{3,4},{4,5},{5,6},{6,7},{7,0},{8,9},{9,10},{10,1... | collective-permute-start | bytes 27656 | tf_op jit(solution)/shard_map/ppermute | solution.py:31
  195.2 1.9 copy-start
